TPU v7x, 32 devices: a whole 2x2x4 slice. The times are simulated.
32 devices in a mesh: rep: 2 (over y), tp: 2 (over x), exp: 8 (over z, core).
Axes of the slice: x: 2, y: 2, z: 4, core: 2. Of those that a mesh axis runs over, the one named last changes fastest.
Arguments:
- attention: bfloat16 [2048, 2048], P(('rep', 'exp'), 'tp'), may hold values from -6 to 6
- stream: bfloat16 [2048, 2048], P(('rep', 'exp'), 'tp'), may hold values from -6 to 6
- proj_weight: bfloat16 [2048, 2048], P(('tp', 'exp')), may hold values from -0.125 to 0.125
- norm_gain: float32 [2048], replicated, may hold values from 0.1 to 1.9
- expert_ids: int32 [2048, 8], P(('rep', 'exp')), may hold values from 0 to 31, all different within a row; in each aligned block of 128 rows (0 to 127, 128 to 255, ...) at most 40 rows name the same one
- gate_fixed: int32 [2048, 8], P(('rep', 'exp')), may hold values from 1 to 65535
- w_gate: bfloat16 [32, 2048, 512], P('exp', None, 'tp'), may hold values from -0.125 to 0.125
- w_up: bfloat16 [32, 2048, 512], P('exp', None, 'tp'), may hold values from -0.125 to 0.125
- w_down: bfloat16 [32, 512, 2048], P('exp', 'tp'), may hold values from -0.25 to 0.25
- gradient: float32 [2, 2048, 2048], P('rep', ('tp', 'exp')), may hold values from -6 to 6
- feedback: float32 [2, 2048, 2048], P('rep', ('tp', 'exp')), may hold values from -4 to 4
- block_ids: int32 [2, 16, 64], P('rep', ('tp', 'exp')), may hold values from 0 to 2047, as said below
Outputs:
- output: bfloat16 [2048, 2048], P(('rep', 'exp'), 'tp')
- update: float32 [2048, 2048], P(('tp', 'exp'))
- new_error: float32 [2, 2048, 2048], P('rep', ('tp', 'exp'))
Inputs may be any that keep to these rules, and one draw needn't show every extreme that they name: `expert_ids`: each row names 8 different experts; within each aligned block of 128 rows no expert is named by more than 40 rows, a bound that some block reaches. `block_ids`: the 64 block numbers of one replica's row group are distinct.
All inputs are finite; a program needn't handle non-finite values.
Results may differ from a plain program's by a relative error of at most 0.0064.
Values may be sent and summed in bfloat16 or wider, within the bound.
No kernel may reach another device: no remote copies, remote signals or barrier semaphores. Data moves between devices by JAX's collectives and lax.ppermute only.
A program may use at most 64 MiB of HBM per device.

v0:
```python
import jax
import jax.numpy as jnp
from jax import lax
from jax.sharding import PartitionSpec as P

EXPERTS = 32
TOP = 8
BLK = 128
CAP = 40


def slot_position(ids_block, experts):
    flat_ids = ids_block.reshape(-1)
    table = (flat_ids[:, None] == jnp.arange(experts, dtype=jnp.int32)[None, :]).astype(jnp.int32)
    before = jnp.cumsum(table, axis=0) - table
    return jnp.sum(before * table, axis=1)


def expert_apply(slots, w_gate, w_up, w_down):
    local_count = w_gate.shape[0]
    senders = slots.shape[0] // local_count
    grouped = slots.reshape(senders, local_count, slots.shape[1], slots.shape[2])
    gate = jnp.einsum("sjcd,jdf->sjcf", grouped, w_gate, preferred_element_type=jnp.float32)
    upper = jnp.einsum("sjcd,jdf->sjcf", grouped, w_up, preferred_element_type=jnp.float32)
    hidden = (jax.nn.silu(gate) * upper).astype(jnp.bfloat16)
    produced = jnp.einsum("sjcf,jfd->sjcd", hidden, w_down, preferred_element_type=jnp.float32)
    return produced.astype(jnp.bfloat16).reshape(slots.shape)


def on_device(
    attention,
    stream,
    proj_weight,
    norm_gain,
    expert_ids,
    gate_fixed,
    w_gate,
    w_up,
    w_down,
    gradient,
    feedback,
    block_ids,
):
    tok_rows = attention.shape[0]
    col_half = stream.shape[1]
    groups_count = lax.axis_size("tp")
    width = col_half * groups_count
    empty = jnp.zeros((tok_rows, width), jnp.float32)
    placed = lax.dynamic_update_slice_in_dim(
        empty, stream.astype(jnp.float32), lax.axis_index("tp") * col_half, 1
    )
    partial_value = placed + jnp.dot(
        attention,
        lax.all_gather(proj_weight, "exp", axis=0, tiled=True),
        preferred_element_type=jnp.float32,
    )
    residual = lax.psum(partial_value, "tp").astype(jnp.bfloat16)
    res_float = residual.astype(jnp.float32)
    scale = lax.rsqrt(jnp.mean(res_float * res_float, axis=1, keepdims=True) + 1e-06)
    normed = (res_float * scale * norm_gain).astype(jnp.bfloat16)
    positions = slot_position(expert_ids, EXPERTS)
    places = expert_ids.reshape(-1) * CAP + positions
    copies = jnp.broadcast_to(normed[:, None, :], (tok_rows, TOP, width)).reshape(
        tok_rows * TOP, width
    )
    outbound = (
        jnp.zeros((EXPERTS * CAP, width), jnp.bfloat16)
        .at[places]
        .set(copies)
        .reshape(EXPERTS, CAP, width)
    )
    results = expert_apply(
        lax.all_to_all(outbound, "exp", split_axis=0, concat_axis=0, tiled=True),
        w_gate,
        w_up,
        w_down,
    )
    pieces = results.reshape(EXPERTS, CAP, groups_count, col_half)
    own_pieces = lax.all_to_all(pieces, "tp", split_axis=2, concat_axis=2, tiled=True)
    slot_sums = jnp.sum(own_pieces.astype(jnp.float32), axis=2).astype(jnp.bfloat16)
    returned = lax.all_to_all(slot_sums, "exp", split_axis=0, concat_axis=0, tiled=True)
    combined = returned.reshape(EXPERTS * CAP, col_half)[places].reshape(tok_rows, TOP, col_half)
    weights = gate_fixed.astype(jnp.float32) / 65536.0
    mixed = jnp.sum(weights[:, :, None] * combined.astype(jnp.float32), axis=1)
    own_cols = lax.dynamic_slice_in_dim(res_float, lax.axis_index("tp") * col_half, col_half, 1)
    output = (own_cols + mixed).astype(jnp.bfloat16)
    accumulated = gradient + feedback
    blocks = accumulated.reshape(-1, BLK)
    chosen = block_ids.reshape(-1)
    values = blocks[chosen]
    all_values, all_chosen = (
        lax.all_gather(values.astype(jnp.bfloat16), "rep", axis=0, tiled=True).astype(values.dtype),
        lax.all_gather(chosen, "rep", axis=0, tiled=True),
    )
    update = jnp.zeros_like(blocks).at[all_chosen].add(all_values) / lax.axis_size("rep")
    remaining = blocks.at[chosen].set(0.0).reshape(accumulated.shape)
    update = update.reshape(accumulated.shape[1], accumulated.shape[2])
    return (output, update, remaining)


def solution(mesh):
    in_specs = (
        P(("rep", "exp"), "tp"),
        P(("rep", "exp"), "tp"),
        P(("tp", "exp"), None),
        P(),
        P(("rep", "exp"), None),
        P(("rep", "exp"), None),
        P("exp", None, "tp"),
        P("exp", None, "tp"),
        P("exp", "tp", None),
        P("rep", ("tp", "exp"), None),
        P("rep", ("tp", "exp"), None),
        P("rep", ("tp", "exp"), None),
    )
    out_specs = (P(("rep", "exp"), "tp"), P(("tp", "exp"), None), P("rep", ("tp", "exp"), None))
    return jax.shard_map(
        on_device, mesh=mesh, in_specs=in_specs, out_specs=out_specs, check_vma=False
    )
```

profile of v0, /device:TPU:0, one launch (start us, length us, event | category | flops | bytes accessed | tf_op | source)
XLA Modules:
  0.0 405.6 jit_solution(2126904307517873067)
XLA Ops:
  8.9 9.0 %reduce-window.6 = s32[32,8,128]{2,1,0:T(8,128)S(1)} reduce-window(s32[32,8,128]{2,1,0:T(8,128)S(1)} %fusion.48, s32[]{:T(128)} %constant.14.clone.1), window={size=1x1x128 pad=0_0x0_0x127_0}, to_apply=%region_1.0 | reduce-window | flops 4161536 | bytes 262148 | tf_op jit(solution)/shard_map/reduce-window
  19.4 39.9 %all-gather.3.cloned.1.call-done = bf16[1024,2048]{1,0:T(8,128)(2,1)} async-done(((bf16[128,2048]{1,0:T(8,128)(2,1)}), bf16[1024,2048]{1,0:T(8,128)(2,1)}) %all-gather.3.cloned.1.call-update) | async-done | bytes 4194320 | tf_op jit(solution)/shard_map/all_gather | solution.py:54
  59.3 2.9 fusion.54
  62.3 29.8 %all-reduce.2 = bf16[128,2048]{1,0:T(8,128)(2,1)S(1)} all-reduce(f32[128,2048]{1,0:T(8,128)S(1)} %add_dynamic-update-slice_fusion), channel_id=1, replica_groups=mesh['rep'=2,'tp'=2,'exp'=8] {'tp'}, use_global_device_ids=true, to_apply=%region_0.0 | all-reduce | flops 262144 | bytes 1572864 | tf_op jit(solution)/shard_map/psum | solution.py:57
  92.5 9.6 %scatter_custom_fusion = bf16[1280,2048]{1,0:T(8,128)(2,1)} fusion(s32[1024]{0:T(1024)S(1)} %bitcast.86, bf16[]{:T(256)} %constant.20.clone.1, bf16[128,2048]{1,0:T(8,128)(2,1)S(1)} %multiply_convert_fusion), kind=kCustom, calls=%fused_computation.16 | custom fusion | bytes 5767170 | tf_op jit(solution)/shard_map/scatter | solution.py:69
  102.1 120.4 %all_to_all.15 = bf16[32,40,2048]{2,1,0:T(8,128)(2,1)S(1)} all-to-all(bf16[32,40,2048]{2,1,0:T(8,128)(2,1)} %bitcast.80), channel_id=1, replica_groups=mesh['rep'=2,'tp'=2,'exp'=8] {'exp'}, dimensions={0} | all-to-all | bytes 10485760 | tf_op jit(solution)/shard_map/all_to_all | solution.py:73
  222.5 2.3 copy-done.2
  226.6 10.3 %convert_bitcast_fusion = bf16[8,4,40,2048]{3,2,0,1:T(8,128)(2,1)} fusion(bf16[4,256,2048]{2,1,0:T(8,128)(2,1)} %param.20, bf16[4,2048,256]{2,1,0:T(8,128)(2,1)} %param.19, bf16[8,4,40,2048]{3,2,1,0:T(8,128)(2,1)} %bitcast.82, f32[8,4,40,256]{3,2,0,1:T(8,128)S(1)} %fusion.15), kind=kOutput, calls=%fused_computation.5 | convolution fusion | flops 2688942080 | bytes 20185088 | tf_op jit(solution)/shard_map/sjcf,jfd->sjcd/dot_general | solution.py:26
  236.9 5.7 %copy.32 = bf16[8,4,40,2048]{3,2,1,0:T(8,128)(2,1)} copy(bf16[8,4,40,2048]{3,2,0,1:T(8,128)(2,1)} %convert_bitcast_fusion) | data formatting | bytes 10485760 | tf_op jit(solution)/shard_map/convert_element_type | solution.py:27
  242.6 9.5 %reshape_reshape.3 = bf16[32,40,2,1024]{3,2,1,0:T(2,128)(2,1)} reshape(bf16[8,4,40,2048]{3,2,1,0:T(8,128)(2,1)} %copy.32) | data formatting | bytes 10485760 | tf_op jit(solution)/shard_map/reshape;reshape | solution.py:78
  252.0 4.1 %copy.33 = bf16[32,40,2,1024]{3,1,0,2:T(8,128)(2,1)S(1)} copy(bf16[32,40,2,1024]{3,2,1,0:T(2,128)(2,1)} %reshape_reshape.3) | data formatting | bytes 10485760 | tf_op jit(solution)/shard_map/reshape;reshape | solution.py:78
  256.2 62.4 %all_to_all.16 = bf16[32,40,2,1024]{3,1,0,2:T(8,128)(2,1)} all-to-all(bf16[32,40,2,1024]{3,1,0,2:T(8,128)(2,1)S(1)} %copy.33), channel_id=1, replica_groups=mesh['rep'=2,'tp'=2,'exp'=8] {'tp'}, dimensions={2} | all-to-all | bytes 10485760 | tf_op jit(solution)/shard_map/all_to_all | solution.py:79
  318.6 6.1 %reduce_sum.44 = bf16[32,40,1024]{2,1,0:T(8,128)(2,1)} reduce(bf16[32,40,2,1024]{3,1,0,2:T(8,128)(2,1)} %all_to_all.16, bf16[]{:T(256)} %constant.20.clone.1), dimensions={2}, to_apply=%region_6.7 | reduce | flops 1310720 | bytes 7864322 | tf_op jit(solution)/shard_map/reduce_sum | solution.py:80
  324.7 3.8 all-to-all-start.2
  328.6 2.6 add.81
  331.2 2.4 reshape.126
  336.7 2.9 scatter_custom_fusion.2
  339.7 4.3 %all-reduce = s32[128]{0:T(128)S(1)} all-reduce(s32[128]{0:T(128)S(1)} %bitcast_dynamic-update-slice_fusion), channel_id=2, replica_groups=mesh['rep'=2,'tp'=2,'exp'=8] {'rep'}, use_global_device_ids=true, to_apply=%add | all-reduce | flops 128 | bytes 1024 | tf_op jit(solution)/shard_map/all_gather | solution.py:93
  343.9 4.4 %all_gather.11 = bf16[128,128]{1,0:T(8,128)(2,1)S(1)} all-gather(bf16[64,128]{1,0:T(8,128)(2,1)S(1)} %gather_fusion.1), channel_id=1, replica_groups=mesh['rep'=2,'tp'=2,'exp'=8] {'rep'}, dimensions={0}, use_global_device_ids=true | all-gather | bytes 49152 | tf_op jit(solution)/shard_map/all_gather | solution.py:92
  352.6 2.4 reshape.128
  355.0 2.4 reshape.129
  358.4 30.3 %all-to-all-done.2 = bf16[32,40,1024]{2,1,0:T(8,128)(2,1)S(1)} async-done(((bf16[32,40,1024]{2,1,0:T(8,128)(2,1)}), bf16[32,40,1024]{2,1,0:T(8,128)(2,1)S(1)}, u32[]{:S(2)}, u32[]{:S(2)}) %all-to-all-start.2) | async-done | bytes 2621472 | tf_op jit(solution)/shard_map/all_to_all | solution.py:81
  388.7 5.4 %gather_fusion = bf16[1024,1024]{1,0:T(8,128)(2,1)} fusion(bf16[1280,1024]{1,0:T(8,128)(2,1)S(1)} %bitcast.79, s32[1024]{0:T(1024)S(1)} %broadcast_clamp_fusion), kind=kCustom, calls=%fused_computation | custom fusion | bytes 4198400 | tf_op jit(solution)/shard_map/gather | solution.py:82
  394.0 2.9 fusion.4
  (53 shorter events, 15.1 us)
Async XLA Ops:
  7.2 52.1 %copy-start = (bf16[128,1024]{1,0:T(8,128)(2,1)S(1)}, bf16[128,1024]{1,0:T(8,128)(2,1)}, u32[]{:S(2)}) copy-start(bf16[128,1024]{1,0:T(8,128)(2,1)} %param.12) | copy-start | bytes 786436
  7.2 55.0 %copy-start.3 = (bf16[128,1024]{1,0:T(8,128)(2,1)S(1)}, bf16[128,1024]{1,0:T(8,128)(2,1)}, u32[]{:S(2)}) copy-start(bf16[128,1024]{1,0:T(8,128)(2,1)} %param.13) | copy-start | bytes 786436
  7.2 52.1 %all-gather.3.cloned.1.call-start = ((), (), s32[]{:S(2)}) async-start(), calls=%async_computation.3 | async-start | bytes 4718592 | tf_op jit(solution)/shard_map/all_gather | solution.py:54
  19.4 73.0 %copy-start.4 = (f32[2048]{0:T(1024)S(1)}, f32[2048]{0:T(1024)}, u32[]{:S(2)}) copy-start(f32[2048]{0:T(1024)} %param.15) | copy-start | bytes 24580
  102.1 122.7 %copy-start.6 = (bf16[4,2048,256]{2,1,0:T(8,128)(2,1)S(1)}, bf16[4,2048,256]{2,1,0:T(8,128)(2,1)}, u32[]{:S(2)}) copy-start(bf16[4,2048,256]{2,1,0:T(8,128)(2,1)} %param.18) | copy-start | bytes 12582916
  222.5 2.3 copy-start.2
  324.7 3.8 copy-start.5
  324.7 8.9 %copy-start.7 = (s32[1,1,64]{2,1,0:T(1,128)S(1)}, s32[1,1,64]{2,1,0:T(1,128)}, u32[]{:S(2)}) copy-start(s32[1,1,64]{2,1,0:T(1,128)} %param.23) | copy-start | bytes 772
  324.7 10.8 %copy-start.8 = (u32[32]{0:T(128)S(1)}, u32[32]{0:T(128)}, u32[]{:S(2)}) copy-start(u32[32]{0:T(128)} %constant.55) | copy-start | bytes 388
  324.7 64.0 %all-to-all-start.2 = ((bf16[32,40,1024]{2,1,0:T(8,128)(2,1)}), bf16[32,40,1024]{2,1,0:T(8,128)(2,1)S(1)}, u32[]{:S(2)}, u32[]{:S(2)}) async-start(bf16[32,40,1024]{2,1,0:T(8,128)(2,1)} %reduce_sum.44), calls=%async_computation.2 | async-start | bytes 5242880 | tf_op jit(solution)/shard_map/all_to_all | solution.py:81
  388.7 10.1 %copy-start.1 = (bf16[128,1024]{1,0:T(8,128)(2,1)S(1)}, bf16[128,1024]{1,0:T(8,128)(2,1)}, u32[]{:S(2)}) copy-start(bf16[128,1024]{1,0:T(8,128)(2,1)} %param.12) | copy-start | bytes 786436
Sparse Core Ops, SparseCore 0:
  9.6 49.6 all-gather.2
where the time goes:
time: 407 us; the launch traced here: 406 us
  blocking collectives  221 us (54%)
  waiting for transfers between devices  70.8 us (17%)
  local copies, waits for them, and re-layouts  50.7 us (12%)
  other arithmetic  29.3 us (7%)
  matrix products  14.9 us (4%)
  between operations  14.9 us (4%)
    all_to_all x1, blocking collectives, on_device(): lax.all_to_all(outbound, 'exp', split_axis=0, concat_axis=0, tiled=True)  120 us
    all_to_all x1, blocking collectives, on_device(): lax.all_to_all(pieces, 'tp', split_axis=2, concat_axis=2, tiled=True)  62.4 us
    all_gather x1, waiting for transfers between devices, on_device(): lax.all_gather(proj_weight, 'exp', axis=0, tiled=True)  39.9 us
    all_to_all x1, waiting for transfers between devices, on_device(): lax.all_to_all(slot_sums, 'exp', split_axis=0, concat_axis=0, tiled=True)  30.3 us
    psum x1, blocking collectives, on_device(): residual = lax.psum(partial_value, 'tp').astype(jnp.bfloat16)  29.8 us
    another operation x2, local copies, waits for them, and re-layouts, on_device(): pieces = results.reshape(EXPERTS, CAP, groups_count, col_half)  13.6 us
    dot_general x1, matrix products, expert_apply(): jnp.einsum('sjcf,jfd->sjcd', hidden, w_down, preferred_element_type=jnp.f...  10.3 us
    scatter x1, local copies, waits for them, and re-layouts, on_device(): outbound = jnp.zeros((EXPERTS * CAP, width), jnp.bfloat16).at[places].set...  9.62 us
  transfers between devices with their start and end apart: 2, of which 2 were waited for; matrix products, arithmetic and copies ran while one was open for 8% of the time, Pallas kernels for 0%

commit v1 on v0

v1 whole, which is shorter than its diff:
```python
import functools

import jax
import jax.numpy as jnp
from jax import lax
from jax.experimental import pallas as pl
from jax.experimental.pallas import tpu as pltpu
from jax.sharding import PartitionSpec as P

EXPERTS = 32
BLK = 128
CORES = 2

F32 = jnp.float32
BF16 = jnp.bfloat16
VMEM = pl.BlockSpec(memory_space=pltpu.VMEM)
SMEM = pl.BlockSpec(memory_space=pltpu.SMEM)


def project_kernel(senders, where_ref, own_ref, far_ref, own_core_ref, far_core_ref, side_ref, side_core_ref, *rest):
    weights, (mine_ref, peer_ref, full_ref) = rest[:senders], rest[senders:]
    rows = weights[0].shape[2]
    core = where_ref[2]
    for turn in range(senders):
        at = where_ref[3 + turn]
        for part in range(2):
            for rel in range(2):
                which = core if rel == 0 else 1 - core
                start = pl.multiple_of((at * CORES + which) * rows, rows)
                full_ref[part, pl.ds(start, rows), :] = weights[turn][part, rel]
    for rel, (near, far, side) in enumerate(
        ((own_ref, far_ref, side_ref), (own_core_ref, far_core_ref, side_core_ref))
    ):
        groups, tok, depth = near.shape
        total = jnp.dot(near[...].reshape(groups * tok, depth), full_ref[0], preferred_element_type=F32)
        total += jnp.dot(far[...].reshape(groups * tok, depth), full_ref[1], preferred_element_type=F32)
        for group, out_ref in enumerate((mine_ref, peer_ref)):
            piece = total[group * tok : (group + 1) * tok] + side[group].astype(F32)
            out_ref[rel] = piece.astype(BF16)


def expert_kernel(
    where_ref, a_ref, b_ref, ac_ref, bc_ref, mix_ref, gain_ref, gate_ref, up_ref, down_ref, keep_ref, send_ref, x_ref, h_ref
):
    x, y, core, home = where_ref[0], where_ref[1], where_ref[2], where_ref[3]
    tok = a_ref.shape[2]
    piece = a_ref.shape[3]
    width = x_ref.shape[1]
    local, ff = gate_ref.shape[0], gate_ref.shape[2]

    def offset(xrel, yrel, crel):
        xx = x if xrel == 0 else 1 - x
        yy = y if yrel == 0 else 1 - y
        cc = core if crel == 0 else 1 - core
        return pl.multiple_of(((xx * 2 + yy) * CORES + cc) * piece, piece)

    for rel in range(2):
        pieces = []
        for xrel, crel, ref in ((0, 0, a_ref), (1, 0, b_ref), (0, 1, ac_ref), (1, 1, bc_ref)):
            for yrel in range(2):
                at = rel if crel == 0 else 1 - rel
                pieces.append((offset(xrel, yrel, crel), ref[yrel, at].astype(F32)))
        square = pieces[0][1] * pieces[0][1]
        for _, value in pieces[1:]:
            square += value * value
        scale = lax.rsqrt(jnp.sum(square, axis=1, keepdims=True) / width + 1e-06)
        for start, value in pieces:
            gain = gain_ref[:, pl.ds(start, piece)]
            x_ref[rel * tok : (rel + 1) * tok, pl.ds(start, piece)] = (value * scale * gain).astype(BF16)
    rows = x_ref[...]
    first = pl.multiple_of((home * CORES + core) * tok, tok)
    second = pl.multiple_of((home * CORES + 1 - core) * tok, tok)
    mix = jnp.concatenate([mix_ref[pl.ds(first, tok), :], mix_ref[pl.ds(second, tok), :]], axis=0)
    for j in range(local):
        gate = jnp.dot(rows, gate_ref[j], preferred_element_type=F32)
        upper = jnp.dot(rows, up_ref[j], preferred_element_type=F32)
        hidden = gate / (1.0 + jnp.exp(-gate)) * upper
        h_ref[:, j * ff : (j + 1) * ff] = (hidden * mix[:, j : j + 1]).astype(BF16)
    inner = h_ref[...]
    half = width // 2
    step = half // 2
    for xrel in range(2):
        xx = x if xrel == 0 else 1 - x
        for part in range(2):
            start = pl.multiple_of(xx * half + part * step, step)
            made = jnp.dot(inner, down_ref[:, pl.ds(start, step)], preferred_element_type=F32)
            keep_ref[xrel, :, part * step : (part + 1) * step] = made[:tok]
            send_ref[xrel, :, part * step : (part + 1) * step] = made[tok:].astype(BF16)


def finish_kernel(count, where_ref, a_ref, ac_ref, *rest):
    parts, out_ref = rest[:count], rest[count]
    y, core = where_ref[1], where_ref[2]
    piece = a_ref.shape[3]
    for yrel in range(2):
        yy = y if yrel == 0 else 1 - y
        for crel, ref in ((0, a_ref), (1, ac_ref)):
            cc = core if crel == 0 else 1 - core
            start = pl.multiple_of((yy * CORES + cc) * piece, piece)
            total = ref[yrel, crel].astype(F32)
            for part in parts:
                total += part[:, pl.ds(start, piece)].astype(F32)
            out_ref[:, pl.ds(start, piece)] = total.astype(BF16)


def cut(value, start, size):
    return lax.dynamic_slice_in_dim(value, start, size, value.ndim - 1)


def turns(count):
    order, low, high = [], 1, count - 1
    while low <= high:
        order.append(low)
        if high != low:
            order.append(high)
        low, high = low + 1, high - 1
    return order


def on_device(
    attention,
    stream,
    proj_weight,
    norm_gain,
    expert_ids,
    gate_fixed,
    w_gate,
    w_up,
    w_down,
    gradient,
    feedback,
    block_ids,
):
    replicas, members = lax.axis_size("rep"), lax.axis_size("exp")
    stack = members // CORES
    x, r, e = lax.axis_index("tp"), lax.axis_index("rep"), lax.axis_index("exp")
    y, z, core = r % 2, e // CORES, e % CORES
    tok, half = stream.shape
    width = half * 2
    quarter, piece = half // 2, half // 4
    local, ff = w_gate.shape[0], w_gate.shape[2]

    over_x = functools.partial(lax.ppermute, axis_name="tp", perm=[(0, 1), (1, 0)])
    over_y = functools.partial(lax.ppermute, axis_name="rep", perm=[(i, i ^ 1) for i in range(replicas)])
    over_core = functools.partial(lax.ppermute, axis_name="exp", perm=[(i, i ^ 1) for i in range(members)])

    def over_z(value, by):
        perm = [(i, (i + by * CORES) % members) for i in range(members)]
        return lax.ppermute(value, "exp", perm)

    place = jnp.stack([x, y, core])
    order = turns(stack)
    homes = [z] + [(z - by) % stack for by in order]

    weight_far = over_x(cut(proj_weight, (1 - x) * half + y * quarter, quarter))
    weight_two = jnp.stack([cut(proj_weight, x * half + y * quarter, quarter), weight_far])
    weight_core = over_core(cut(weight_two, (1 - core) * piece, piece))
    weight_block = jnp.stack([cut(weight_two, core * piece, piece), weight_core], axis=1)
    blocks = [weight_block] + [over_z(weight_block, by) for by in order]

    sent = jnp.concatenate([attention, cut(stream, (1 - y) * quarter, quarter)], axis=1)
    came = over_y(sent)
    near = jnp.stack([attention, came[:, :half]])
    side = jnp.stack([cut(stream, y * quarter, quarter), came[:, half:]])
    far = over_x(near)
    near_core, far_core = over_core(near), over_core(far)
    side_core = over_core(cut(side, (1 - core) * piece, piece))
    side = cut(side, core * piece, piece)

    ids, fixed = expert_ids.T, gate_fixed.T.astype(F32) / 65536.0
    named = ids[:, None, :] == jnp.arange(EXPERTS, dtype=jnp.int32)[None, :, None]
    table = jnp.sum(jnp.where(named, fixed[:, None, :], 0.0), axis=0)
    table = lax.all_to_all(table, "exp", split_axis=0, concat_axis=0, tiled=True)
    mix = table.reshape(members, local, tok).transpose(0, 2, 1).reshape(members * tok, local)

    slab = jax.ShapeDtypeStruct((2, tok, piece), BF16)
    mine, peer = pl.pallas_call(
        functools.partial(project_kernel, stack),
        in_specs=[SMEM] + [VMEM] * (6 + stack),
        out_specs=(VMEM, VMEM),
        out_shape=(slab, slab),
        scratch_shapes=[pltpu.VMEM((2, half, piece), BF16)],
        name="project",
    )(jnp.concatenate([place, jnp.stack(homes)]), near, far, near_core, far_core, side, side_core, *blocks)
    rows = jnp.stack([mine, over_y(peer)])

    gain = norm_gain.reshape(1, width)
    down = w_down.reshape(local * ff, width)

    def run(home, a):
        b = over_x(a)
        ac, bc = over_core(a), over_core(b)
        keep, send = pl.pallas_call(
            expert_kernel,
            in_specs=[SMEM] + [VMEM] * 9,
            out_specs=(VMEM, VMEM),
            out_shape=(
                jax.ShapeDtypeStruct((2, tok, half), F32),
                jax.ShapeDtypeStruct((2, tok, half), BF16),
            ),
            scratch_shapes=[pltpu.VMEM((2 * tok, width), BF16), pltpu.VMEM((2 * tok, local * ff), BF16)],
            name="experts",
        )(jnp.concatenate([place, home[None]]), a, b, ac, bc, mix, gain, w_gate, w_up, down)
        other = over_core(send).astype(F32)
        beyond = over_x((keep[1] + other[1]).astype(BF16)).astype(F32)
        return keep[0] + other[0] + beyond, ac

    arrived = [over_z(rows, by) for by in order]
    total, rows_core = run(z, rows)
    parts = [total]
    for by, home, block in zip(order, homes[1:], arrived):
        made, _ = run(home, block)
        parts.append(over_z(made.astype(BF16), -by))
    output = pl.pallas_call(
        functools.partial(finish_kernel, len(parts)),
        in_specs=[SMEM] + [VMEM] * (2 + len(parts)),
        out_specs=VMEM,
        out_shape=jax.ShapeDtypeStruct((tok, half), BF16),
        name="finish",
    )(place, rows, rows_core, *parts)

    accumulated = (gradient + feedback)[0]
    height, depth = accumulated.shape
    across = depth // BLK
    chosen = block_ids.reshape(-1)
    row_hit = (jnp.arange(height, dtype=jnp.int32)[:, None] == chosen[None, :] // across).astype(BF16)
    col_hit = (jnp.arange(depth, dtype=jnp.int32)[None, :] // BLK == chosen[:, None] % across).astype(BF16)
    hit = jnp.dot(row_hit, col_hit, preferred_element_type=F32) > 0.5
    picked = jnp.where(hit, accumulated, 0.0)
    remaining = jnp.where(hit, 0.0, accumulated)[None]
    moved = picked.astype(BF16)
    update = picked
    for by in range(1, replicas):
        perm = [(i, (i + by) % replicas) for i in range(replicas)]
        update = update + lax.ppermute(moved, "rep", perm).astype(F32)
    return (output, update / replicas, remaining)


def solution(mesh):
    in_specs = (
        P(("rep", "exp"), "tp"),
        P(("rep", "exp"), "tp"),
        P(("tp", "exp"), None),
        P(),
        P(("rep", "exp"), None),
        P(("rep", "exp"), None),
        P("exp", None, "tp"),
        P("exp", None, "tp"),
        P("exp", "tp", None),
        P("rep", ("tp", "exp"), None),
        P("rep", ("tp", "exp"), None),
        P("rep", ("tp", "exp"), None),
    )
    out_specs = (P(("rep", "exp"), "tp"), P(("tp", "exp"), None), P("rep", ("tp", "exp"), None))
    return jax.shard_map(
        on_device, mesh=mesh, in_specs=in_specs, out_specs=out_specs, check_vma=False
    )
```

time: 407 us -> 197 us (0.48)
  blocking collectives: 221 us -> 0 us
  Pallas kernels: 0 us -> 46.6 us
  local copies, waits for them, and re-layouts: 50.7 us -> 8.84 us
  starting transfers between devices: 3.8 us -> 37 us
  waiting for transfers between devices: 70.8 us -> 89.1 us
  other arithmetic: 29.3 us -> 13 us
  between operations: 14.9 us -> 1.03 us
  matrix products: 14.9 us -> 1.23 us
    all_to_all x2 -> x0, blocking collectives: 183 us -> none  [the longest x1 120 us: on_device(): lax.all_to_all(outbound, 'exp', split_axis=0, concat_axis=0, tiled=True)]
    ppermute x0 -> x38, waiting for transfers between devices: none -> 87 us  [the longest x9 44 us: over_z(): return lax.ppermute(value, 'exp', perm)]
    pallas_call x0 -> x6, Pallas kernels: none -> 46.6 us  [the longest x4 41 us: run(): pl.pallas_call(expert_kernel, in_specs=[SMEM] + [VMEM] * 9, out_specs=(VM...]
    all_gather x1 -> x0, waiting for transfers between devices: 39.9 us -> none  [on_device(): lax.all_gather(proj_weight, 'exp', axis=0, tiled=True)]
    ppermute x0 -> x38, starting transfers between devices: none -> 30.3 us  [the longest x9 9.41 us: over_z(): return lax.ppermute(value, 'exp', perm)]
    psum x1 -> x0, blocking collectives: 29.8 us -> none  [on_device(): residual = lax.psum(partial_value, 'tp').astype(jnp.bfloat16)]
    all_to_all x1, waiting for transfers between devices: 30.3 us -> 2.15 us  [on_device(): lax.all_to_all(table, 'exp', split_axis=0, concat_axis=0, tiled=True)]
    dot_general x3 -> x1, matrix products: 14.9 us -> 1.23 us  [on_device(): hit = jnp.dot(row_hit, col_hit, preferred_element_type=F32) > 0.5]
  transfers between devices with their start and end apart: 2 -> 39, of which waited for: 2 -> 14; matrix products, arithmetic and copies ran while one was open for 8% -> 8% of each run, Pallas kernels for 0% -> 21%
where the time goes in v1:
time: 197 us
  waiting for transfers between devices  89.1 us (45%)
  Pallas kernels  46.6 us (24%)
  starting transfers between devices  37 us (19%)
  other arithmetic  13 us (7%)
  local copies, waits for them, and re-layouts  8.84 us (4%)
    ppermute x9, waiting for transfers between devices, over_z(): return lax.ppermute(value, 'exp', perm)  44 us
    pallas_call x4, Pallas kernels, run(): pl.pallas_call(expert_kernel, in_specs=[SMEM] + [VMEM] * 9, out_specs=(VM...  41 us
    ppermute x4, waiting for transfers between devices, run(): beyond = over_x((keep[1] + other[1]).astype(BF16)).astype(F32)  16.8 us
    ppermute x1, waiting for transfers between devices, on_device(): weight_far = over_x(cut(proj_weight, (1 - x) * half + y * quarter, quarter))  12.2 us
    ppermute x9, starting transfers between devices, over_z(): return lax.ppermute(value, 'exp', perm)  9.41 us
    ppermute x1, waiting for transfers between devices, on_device(): came = over_y(sent)  9.11 us
    all_to_all x1, starting transfers between devices, on_device(): lax.all_to_all(table, 'exp', split_axis=0, concat_axis=0, tiled=True)  6.71 us
    ppermute x4, starting transfers between devices, run(): b = over_x(a)  4.91 us
  transfers between devices with their start and end apart: 39, of which 14 were waited for; matrix products, arithmetic and copies ran while one was open for 8% of the time, Pallas kernels for 21%

profile of v1, /device:TPU:0, one launch (start us, length us, event | category | flops | bytes accessed | tf_op | source)
XLA Modules:
  0.0 196.9 jit_solution(8943644509188962497)
XLA Ops:
  2.7 3.1 %collective-permute-start = (bf16[128,1536]{1,0:T(8,128)(2,1)S(1)}, bf16[128,1536]{1,0:T(8,128)(2,1)S(1)}, u32[]{:S(2)}, u32[]{:S(2)}) collective-permute-start(bf16[128,1536]{1,0:T(8,128)(2,1)S(1)} %pad_maximum_fusion.1), channel_id=1, source_target_pairs={{0,16},{16,0},{1,17},{17,1},{2,18},{18,2},{3,19},{19,3},{4,20},{20... | collective-permute-start | bytes 1179656 | tf_op jit(solution)/shard_map/ppermute | solution.py:162
  5.7 9.1 %collective-permute-done = bf16[128,1536]{1,0:T(8,128)(2,1)S(1)} collective-permute-done((bf16[128,1536]{1,0:T(8,128)(2,1)S(1)}, bf16[128,1536]{1,0:T(8,128)(2,1)S(1)}, u32[]{:S(2)}, u32[]{:S(2)}) %collective-permute-start) | collective-permute-done | bytes 393248 | tf_op jit(solution)/shard_map/ppermute | solution.py:162
  16.6 1.8 collective-permute-start.1
  20.3 12.2 %collective-permute-done.5 = bf16[128,512]{1,0:T(8,128)(2,1)S(1)} collective-permute-done((bf16[128,512]{1,0:T(8,128)(2,1)}, bf16[128,512]{1,0:T(8,128)(2,1)S(1)}, u32[]{:S(2)}, u32[]{:S(2)}) %collective-permute-start.5) | collective-permute-done | bytes 131104 | tf_op jit(solution)/shard_map/ppermute | solution.py:155
  35.6 2.3 %collective-permute-start.8 = (bf16[2,2,128,256]{3,2,1,0:T(8,128)(2,1)S(1)}, bf16[2,2,128,256]{3,2,1,0:T(8,128)(2,1)}, u32[]{:S(2)}, u32[]{:S(2)}) collective-permute-start(bf16[2,2,128,256]{3,2,1,0:T(8,128)(2,1)S(1)} %pad_maximum_fusion.2.rest_0_), channel_id=1, source_target_pairs={{0,6},{1,7},{2,0},{3,1},{4,2},{5,3},{6,4},{7,5},{8,14},{9,15},{10,... | collective-permute-start | bytes 786440 | tf_op jit(solution)/shard_map/ppermute | solution.py:149
  40.3 4.8 %collective-permute-done.7.rest_1_ = bf16[2,2,128,256]{3,2,1,0:T(8,128)(2,1)S(1)} collective-permute-done((bf16[2,2,128,256]{3,2,1,0:T(8,128)(2,1)S(1)}, bf16[2,2,128,256]{3,2,1,0:T(8,128)(2,1)S(1)}, u32[]{:S(2)}, u32[]{:S(2)}) %collective-permute-start.7) | collective-permute-done | bytes 262176 | tf_op jit(solution)/shard_map/ppermute | solution.py:149
  46.5 3.0 %collective-permute-done.8.rest_2_ = bf16[2,2,128,256]{3,2,1,0:T(8,128)(2,1)} collective-permute-done((bf16[2,2,128,256]{3,2,1,0:T(8,128)(2,1)S(1)}, bf16[2,2,128,256]{3,2,1,0:T(8,128)(2,1)}, u32[]{:S(2)}, u32[]{:S(2)}) %collective-permute-start.8) | collective-permute-done | bytes 262176 | tf_op jit(solution)/shard_map/ppermute | solution.py:149
  49.4 11.8 %collective-permute-done.9.rest_3_ = bf16[2,2,128,256]{3,2,1,0:T(8,128)(2,1)} collective-permute-done((bf16[2,2,128,256]{3,2,1,0:T(8,128)(2,1)S(1)}, bf16[2,2,128,256]{3,2,1,0:T(8,128)(2,1)}, u32[]{:S(2)}, u32[]{:S(2)}) %collective-permute-start.9) | collective-permute-done | bytes 262176 | tf_op jit(solution)/shard_map/ppermute | solution.py:149
  61.9 3.4 %project.1 = (bf16[2,128,256]{2,1,0:T(8,128)(2,1)}, bf16[2,128,256]{2,1,0:T(8,128)(2,1)}) custom-call(s32[7]{0:T(128)} %concatenate.23.where_ref, bf16[2,128,1024]{2,1,0:T(8,128)(2,1)} %copy-done.3, bf16[2,128,1024]{2,1,0:T(8,128)(2,1)} %copy-done.10, bf16[2,128,1024]{2,1,0:T(8,128)(2,1)} %collective-permute-done.2.own_core_ref, ...), custom_call_target="tpu_custom_call" | custom-call | tf_op jit(solution)/shard_map/project/pallas_call | solution.py:177
  66.8 4.1 %collective-permute-done.10 = bf16[2,128,256]{2,1,0:T(8,128)(2,1)S(1)} collective-permute-done((bf16[2,128,256]{2,1,0:T(8,128)(2,1)}, bf16[2,128,256]{2,1,0:T(8,128)(2,1)S(1)}, u32[]{:S(2)}, u32[]{:S(2)}) %collective-permute-start.10) | collective-permute-done | bytes 131104 | tf_op jit(solution)/shard_map/ppermute | solution.py:185
  76.7 12.7 %collective-permute-done.30.a_ref = bf16[2,2,128,256]{3,2,1,0:T(8,128)(2,1)} collective-permute-done((bf16[2,2,128,256]{3,2,1,0:T(8,128)(2,1)S(1)}, bf16[2,2,128,256]{3,2,1,0:T(8,128)(2,1)}, u32[]{:S(2)}, u32[]{:S(2)}) %collective-permute-start.30) | collective-permute-done | bytes 262176 | tf_op jit(solution)/shard_map/ppermute | solution.py:149
  94.6 6.7 %all-to-all-start = ((f32[8,4,128]{2,1,0:T(4,128)}), f32[8,4,128]{2,1,0:T(4,128)S(1)}, u32[]{:S(2)}, u32[]{:S(2)}) async-start(f32[8,4,128]{2,1,0:T(4,128)} %bitcast.19), calls=%async_computation | async-start | bytes 32768 | tf_op jit(solution)/shard_map/all_to_all | solution.py:173
  104.9 2.1 %all-to-all-done = f32[8,4,128]{2,1,0:T(4,128)S(1)} async-done(((f32[8,4,128]{2,1,0:T(4,128)}), f32[8,4,128]{2,1,0:T(4,128)S(1)}, u32[]{:S(2)}, u32[]{:S(2)}) %all-to-all-start) | async-done | bytes 16416 | tf_op jit(solution)/shard_map/all_to_all | solution.py:173
  108.0 10.2 %experts.4 = (f32[2,128,1024]{2,1,0:T(8,128)}, bf16[2,128,1024]{2,1,0:T(8,128)(2,1)}) custom-call(s32[4]{0:T(128)} %get-tuple-element.39.where_ref, bf16[2,2,128,256]{3,2,1,0:T(8,128)(2,1)} %copy-done.2, bf16[2,2,128,256]{3,2,1,0:T(8,128)(2,1)} %collective-permute-done.12.b_ref, bf16[2,2,128,256]{3,2,1,0:T(8,128)(2,1)} %copy-done.9, ...), custom_call_target="tpu_custom_call" | custom-call | tf_op jit(solution)/shard_map/experts/pallas_call | solution.py:193
  118.2 10.2 %experts.7 = (f32[2,128,1024]{2,1,0:T(8,128)}, bf16[2,128,1024]{2,1,0:T(8,128)(2,1)}) custom-call(s32[4]{0:T(128)} %get-tuple-element.23.where_ref, bf16[2,2,128,256]{3,2,1,0:T(8,128)(2,1)} %collective-permute-done.30.a_ref, bf16[2,2,128,256]{3,2,1,0:T(8,128)(2,1)} %collective-permute-done.31.b_ref, bf16[2,2,128,256]{3,2,1,0:T(8,128)(2,1)} %collective-permute-done.32.ac_ref, ...), custom_call_target="tpu_custom_call" | custom-call | tf_op jit(solution)/shard_map/experts/pallas_call | solution.py:193
  129.4 10.1 %experts.6 = (f32[2,128,1024]{2,1,0:T(8,128)}, bf16[2,128,1024]{2,1,0:T(8,128)(2,1)}) custom-call(s32[4]{0:T(128)} %get-tuple-element.37.where_ref, bf16[2,2,128,256]{3,2,1,0:T(8,128)(2,1)} %collective-permute-done.23.a_ref, bf16[2,2,128,256]{3,2,1,0:T(8,128)(2,1)} %collective-permute-done.24.b_ref, bf16[2,2,128,256]{3,2,1,0:T(8,128)(2,1)} %collective-permute-done.25.ac_ref, ...), custom_call_target="tpu_custom_call" | custom-call | tf_op jit(solution)/shard_map/experts/pallas_call | solution.py:193
  139.6 1.7 fusion
  142.1 10.5 %experts.5 = (f32[2,128,1024]{2,1,0:T(8,128)}, bf16[2,128,1024]{2,1,0:T(8,128)(2,1)}) custom-call(s32[4]{0:T(128)} %get-tuple-element.38.where_ref, bf16[2,2,128,256]{3,2,1,0:T(8,128)(2,1)} %copy-done.16, bf16[2,2,128,256]{3,2,1,0:T(8,128)(2,1)} %collective-permute-done.17.b_ref, bf16[2,2,128,256]{3,2,1,0:T(8,128)(2,1)} %copy-done.17, ...), custom_call_target="tpu_custom_call" | custom-call | tf_op jit(solution)/shard_map/experts/pallas_call | solution.py:193
  161.5 7.9 %collective-permute-done.35 = bf16[128,1024]{1,0:T(8,128)(2,1)S(1)} collective-permute-done((bf16[128,1024]{1,0:T(8,128)(2,1)S(1)}, bf16[128,1024]{1,0:T(8,128)(2,1)S(1)}, u32[]{:S(2)}, u32[]{:S(2)}) %collective-permute-start.35) | collective-permute-done | bytes 262176 | tf_op jit(solution)/shard_map/ppermute | solution.py:205
  170.1 4.9 %collective-permute-done.28 = bf16[128,1024]{1,0:T(8,128)(2,1)S(1)} collective-permute-done((bf16[128,1024]{1,0:T(8,128)(2,1)S(1)}, bf16[128,1024]{1,0:T(8,128)(2,1)S(1)}, u32[]{:S(2)}, u32[]{:S(2)}) %collective-permute-start.28) | collective-permute-done | bytes 262176 | tf_op jit(solution)/shard_map/ppermute | solution.py:205
  175.7 4.0 %collective-permute-done.21 = bf16[128,1024]{1,0:T(8,128)(2,1)S(1)} collective-permute-done((bf16[128,1024]{1,0:T(8,128)(2,1)S(1)}, bf16[128,1024]{1,0:T(8,128)(2,1)S(1)}, u32[]{:S(2)}, u32[]{:S(2)}) %collective-permute-start.21) | collective-permute-done | bytes 262176 | tf_op jit(solution)/shard_map/ppermute | solution.py:205
  182.1 6.3 %collective-permute-done.36.rest_3_ = bf16[128,1024]{1,0:T(8,128)(2,1)S(1)} collective-permute-done((bf16[128,1024]{1,0:T(8,128)(2,1)S(1)}, bf16[128,1024]{1,0:T(8,128)(2,1)S(1)}, u32[]{:S(2)}, u32[]{:S(2)}) %collective-permute-start.36) | collective-permute-done | bytes 262176 | tf_op jit(solution)/shard_map/ppermute | solution.py:149
  188.4 5.4 %collective-permute-done.22.rest_1_ = bf16[128,1024]{1,0:T(8,128)(2,1)S(1)} collective-permute-done((bf16[128,1024]{1,0:T(8,128)(2,1)S(1)}, bf16[128,1024]{1,0:T(8,128)(2,1)S(1)}, u32[]{:S(2)}, u32[]{:S(2)}) %collective-permute-start.22) | collective-permute-done | bytes 262176 | tf_op jit(solution)/shard_map/ppermute | solution.py:149
  194.5 2.3 %finish.1 = bf16[128,1024]{1,0:T(8,128)(2,1)} custom-call(s32[3]{0:T(128)} %pad_add_fusion.where_ref, bf16[2,2,128,256]{3,2,1,0:T(8,128)(2,1)} %copy-done.2, bf16[2,2,128,256]{3,2,1,0:T(8,128)(2,1)} %copy-done.9, f32[128,1024]{1,0:T(8,128)} %fusion.16.rest_0_, bf16[128,1024]{1,0:T(8,128)(2,1)} %copy-done.15, bf16[128,1024]{1,0:T(8,128)(2,1)} %copy-done.14, ...), custom_call_target="tpu_custom_call" | custom-call | tf_op jit(solution)/shard_map/finish/pallas_call | solution.py:214
  (139 shorter events, 45.4 us)
Async XLA Ops:
  16.6 16.6 %collective-permute-start.1 = (bf16[2,128,1024]{2,1,0:T(8,128)(2,1)S(1)}, bf16[2,128,1024]{2,1,0:T(8,128)(2,1)S(1)}, u32[]{:S(2)}, u32[]{:S(2)}) collective-permute-start(bf16[2,128,1024]{2,1,0:T(8,128)(2,1)S(1)} %pad_maximum_fusion.own_ref), channel_id=1, source_target_pairs={{0,8},{8,0},{1,9},{9,1},{2,10},{10,2},{3,11},{11,3},{4,12},{12,4},... | collective-permute-start | bytes 1572872 | tf_op jit(solution)/shard_map/ppermute | solution.py:165
  32.7 28.6 %collective-permute-start.2 = (bf16[2,128,1024]{2,1,0:T(8,128)(2,1)S(1)}, bf16[2,128,1024]{2,1,0:T(8,128)(2,1)}, u32[]{:S(2)}, u32[]{:S(2)}) collective-permute-start(bf16[2,128,1024]{2,1,0:T(8,128)(2,1)S(1)} %pad_maximum_fusion.own_ref), channel_id=1, source_target_pairs={{0,1},{1,0},{2,3},{3,2},{4,5},{5,4},{6,7},{7,6},{8,9},{9,8},{10,11... | collective-permute-start | bytes 1572872 | tf_op jit(solution)/shard_map/ppermute | solution.py:166
  33.2 28.1 %collective-permute-start.3 = (bf16[2,128,1024]{2,1,0:T(8,128)(2,1)S(1)}, bf16[2,128,1024]{2,1,0:T(8,128)(2,1)}, u32[]{:S(2)}, u32[]{:S(2)}) collective-permute-start(bf16[2,128,1024]{2,1,0:T(8,128)(2,1)S(1)} %collective-permute-done.1.far_ref), channel_id=1, source_target_pairs={{0,1},{1,0},{2,3},{3,2},{4,5},{5,4},{6,7},{7,6},{8,9},{9,8},{10,11... | collective-permute-start | bytes 1572872 | tf_op jit(solution)/shard_map/ppermute | solution.py:166
  38.0 23.3 %collective-permute-start.9 = (bf16[2,2,128,256]{3,2,1,0:T(8,128)(2,1)S(1)}, bf16[2,2,128,256]{3,2,1,0:T(8,128)(2,1)}, u32[]{:S(2)}, u32[]{:S(2)}) collective-permute-start(bf16[2,2,128,256]{3,2,1,0:T(8,128)(2,1)S(1)} %pad_maximum_fusion.2.rest_0_), channel_id=1, source_target_pairs={{0,4},{1,5},{2,6},{3,7},{4,0},{5,1},{6,2},{7,3},{8,12},{9,13},{10,... | collective-permute-start | bytes 786440 | tf_op jit(solution)/shard_map/ppermute | solution.py:149
  45.9 15.4 %collective-permute-start.4 = (bf16[2,128,256]{2,1,0:T(8,128)(2,1)}, bf16[2,128,256]{2,1,0:T(8,128)(2,1)S(1)}, u32[]{:S(2)}, u32[]{:S(2)}) collective-permute-start(bf16[2,128,256]{2,1,0:T(8,128)(2,1)} %get-tuple-element.31), channel_id=1, source_target_pairs={{0,1},{1,0},{2,3},{3,2},{4,5},{5,4},{6,7},{7,6},{8,9},{9,8},{10,11... | collective-permute-start | bytes 393224 | tf_op jit(solution)/shard_map/ppermute | solution.py:167
  71.8 17.6 %collective-permute-start.30 = (bf16[2,2,128,256]{3,2,1,0:T(8,128)(2,1)S(1)}, bf16[2,2,128,256]{3,2,1,0:T(8,128)(2,1)}, u32[]{:S(2)}, u32[]{:S(2)}) collective-permute-start(bf16[2,2,128,256]{3,2,1,0:T(8,128)(2,1)S(1)} %pad_maximum_fusion.3.a_ref), channel_id=1, source_target_pairs={{0,4},{1,5},{2,6},{3,7},{4,0},{5,1},{6,2},{7,3},{8,12},{9,13},{10,... | collective-permute-start | bytes 786440 | tf_op jit(solution)/shard_map/ppermute | solution.py:149
  71.9 19.0 %collective-permute-start.23 = (bf16[2,2,128,256]{3,2,1,0:T(8,128)(2,1)S(1)}, bf16[2,2,128,256]{3,2,1,0:T(8,128)(2,1)}, u32[]{:S(2)}, u32[]{:S(2)}) collective-permute-start(bf16[2,2,128,256]{3,2,1,0:T(8,128)(2,1)S(1)} %pad_maximum_fusion.3.a_ref), channel_id=1, source_target_pairs={{0,6},{1,7},{2,0},{3,1},{4,2},{5,3},{6,4},{7,5},{8,14},{9,15},{10,... | collective-permute-start | bytes 786440 | tf_op jit(solution)/shard_map/ppermute | solution.py:149
  73.1 17.7 %collective-permute-start.16 = (bf16[2,2,128,256]{3,2,1,0:T(8,128)(2,1)S(1)}, bf16[2,2,128,256]{3,2,1,0:T(8,128)(2,1)S(1)}, u32[]{:S(2)}, u32[]{:S(2)}) collective-permute-start(bf16[2,2,128,256]{3,2,1,0:T(8,128)(2,1)S(1)} %pad_maximum_fusion.3.a_ref), channel_id=1, source_target_pairs={{0,2},{1,3},{2,4},{3,5},{4,6},{5,7},{6,0},{7,1},{8,10},{9,11},{10,... | collective-permute-start | bytes 786440 | tf_op jit(solution)/shard_map/ppermute | solution.py:149
  74.0 18.3 %collective-permute-start.12 = (bf16[2,2,128,256]{3,2,1,0:T(8,128)(2,1)S(1)}, bf16[2,2,128,256]{3,2,1,0:T(8,128)(2,1)}, u32[]{:S(2)}, u32[]{:S(2)}) collective-permute-start(bf16[2,2,128,256]{3,2,1,0:T(8,128)(2,1)S(1)} %pad_maximum_fusion.3.a_ref), channel_id=1, source_target_pairs={{0,8},{8,0},{1,9},{9,1},{2,10},{10,2},{3,11},{11,3},{4,12},{12,4},... | collective-permute-start | bytes 786440 | tf_op jit(solution)/shard_map/ppermute | solution.py:191
  75.5 16.9 %collective-permute-start.11 = (bf16[2,2,128,256]{3,2,1,0:T(8,128)(2,1)S(1)}, bf16[2,2,128,256]{3,2,1,0:T(8,128)(2,1)S(1)}, u32[]{:S(2)}, u32[]{:S(2)}) collective-permute-start(bf16[2,2,128,256]{3,2,1,0:T(8,128)(2,1)S(1)} %pad_maximum_fusion.3.a_ref), channel_id=1, source_target_pairs={{0,1},{1,0},{2,3},{3,2},{4,5},{5,4},{6,7},{7,6},{8,9},{9,8},{10,11... | collective-permute-start | bytes 786440 | tf_op jit(solution)/shard_map/ppermute | solution.py:192
  92.4 47.1 %collective-permute-start.37 = (bf16[128,2048]{1,0:T(8,128)(2,1)}, bf16[128,2048]{1,0:T(8,128)(2,1)S(1)}, u32[]{:S(2)}, u32[]{:S(2)}) collective-permute-start(bf16[128,2048]{1,0:T(8,128)(2,1)} %get-tuple-element.40), channel_id=1, source_target_pairs={{0,16},{16,0},{1,17},{17,1},{2,18},{18,2},{3,19},{19,3},{4,20},{20... | collective-permute-start | bytes 1572872 | tf_op jit(solution)/shard_map/ppermute | solution.py:235
  102.0 26.4 %collective-permute-start.25 = (bf16[2,2,128,256]{3,2,1,0:T(8,128)(2,1)}, bf16[2,2,128,256]{3,2,1,0:T(8,128)(2,1)}, u32[]{:S(2)}, u32[]{:S(2)}) collective-permute-start(bf16[2,2,128,256]{3,2,1,0:T(8,128)(2,1)} %collective-permute-done.23.a_ref), channel_id=1, source_target_pairs={{0,1},{1,0},{2,3},{3,2},{4,5},{5,4},{6,7},{7,6},{8,9},{9,8},{10,11... | collective-permute-start | bytes 786440 | tf_op jit(solution)/shard_map/ppermute | solution.py:192
  102.5 26.4 %collective-permute-start.17 = (bf16[2,2,128,256]{3,2,1,0:T(8,128)(2,1)}, bf16[2,2,128,256]{3,2,1,0:T(8,128)(2,1)}, u32[]{:S(2)}, u32[]{:S(2)}) collective-permute-start(bf16[2,2,128,256]{3,2,1,0:T(8,128)(2,1)} %copy-done.16), channel_id=1, source_target_pairs={{0,8},{8,0},{1,9},{9,1},{2,10},{10,2},{3,11},{11,3},{4,12},{12,4},... | collective-permute-start | bytes 786440 | tf_op jit(solution)/shard_map/ppermute | solution.py:191
  103.1 15.1 %collective-permute-start.33 = (bf16[2,2,128,256]{3,2,1,0:T(8,128)(2,1)}, bf16[2,2,128,256]{3,2,1,0:T(8,128)(2,1)}, u32[]{:S(2)}, u32[]{:S(2)}) collective-permute-start(bf16[2,2,128,256]{3,2,1,0:T(8,128)(2,1)} %collective-permute-done.31.b_ref), channel_id=1, source_target_pairs={{0,1},{1,0},{2,3},{3,2},{4,5},{5,4},{6,7},{7,6},{8,9},{9,8},{10,11... | collective-permute-start | bytes 786440 | tf_op jit(solution)/shard_map/ppermute | solution.py:192
  103.1 25.9 %collective-permute-start.26 = (bf16[2,2,128,256]{3,2,1,0:T(8,128)(2,1)}, bf16[2,2,128,256]{3,2,1,0:T(8,128)(2,1)}, u32[]{:S(2)}, u32[]{:S(2)}) collective-permute-start(bf16[2,2,128,256]{3,2,1,0:T(8,128)(2,1)} %collective-permute-done.24.b_ref), channel_id=1, source_target_pairs={{0,1},{1,0},{2,3},{3,2},{4,5},{5,4},{6,7},{7,6},{8,9},{9,8},{10,11... | collective-permute-start | bytes 786440 | tf_op jit(solution)/shard_map/ppermute | solution.py:192
  118.2 23.1 %collective-permute-start.18 = (bf16[2,2,128,256]{3,2,1,0:T(8,128)(2,1)}, bf16[2,2,128,256]{3,2,1,0:T(8,128)(2,1)S(1)}, u32[]{:S(2)}, u32[]{:S(2)}) collective-permute-start(bf16[2,2,128,256]{3,2,1,0:T(8,128)(2,1)} %copy-done.16), channel_id=1, source_target_pairs={{0,1},{1,0},{2,3},{3,2},{4,5},{5,4},{6,7},{7,6},{8,9},{9,8},{10,11... | collective-permute-start | bytes 786440 | tf_op jit(solution)/shard_map/ppermute | solution.py:192
  128.4 24.8 %collective-permute-start.14 = (bf16[2,128,1024]{2,1,0:T(8,128)(2,1)}, bf16[2,128,1024]{2,1,0:T(8,128)(2,1)}, u32[]{:S(2)}, u32[]{:S(2)}) collective-permute-start(bf16[2,128,1024]{2,1,0:T(8,128)(2,1)} %get-tuple-element.16), channel_id=1, source_target_pairs={{0,1},{1,0},{2,3},{3,2},{4,5},{5,4},{6,7},{7,6},{8,9},{9,8},{10,11... | collective-permute-start | bytes 1572872 | tf_op jit(solution)/shard_map/ppermute | solution.py:204
  128.9 26.2 %collective-permute-start.34 = (bf16[2,128,1024]{2,1,0:T(8,128)(2,1)}, bf16[2,128,1024]{2,1,0:T(8,128)(2,1)}, u32[]{:S(2)}, u32[]{:S(2)}) collective-permute-start(bf16[2,128,1024]{2,1,0:T(8,128)(2,1)} %get-tuple-element.22), channel_id=1, source_target_pairs={{0,1},{1,0},{2,3},{3,2},{4,5},{5,4},{6,7},{7,6},{8,9},{9,8},{10,11... | collective-permute-start | bytes 1572872 | tf_op jit(solution)/shard_map/ppermute | solution.py:204
  139.5 18.4 %collective-permute-start.27 = (bf16[2,128,1024]{2,1,0:T(8,128)(2,1)}, bf16[2,128,1024]{2,1,0:T(8,128)(2,1)}, u32[]{:S(2)}, u32[]{:S(2)}) collective-permute-start(bf16[2,128,1024]{2,1,0:T(8,128)(2,1)} %get-tuple-element.20), channel_id=1, source_target_pairs={{0,1},{1,0},{2,3},{3,2},{4,5},{5,4},{6,7},{7,6},{8,9},{9,8},{10,11... | collective-permute-start | bytes 1572872 | tf_op jit(solution)/shard_map/ppermute | solution.py:204
  154.5 26.7 %collective-permute-start.15 = (bf16[128,1024]{1,0:T(8,128)(2,1)S(1)}, bf16[128,1024]{1,0:T(8,128)(2,1)S(1)}, u32[]{:S(2)}, u32[]{:S(2)}) collective-permute-start(bf16[128,1024]{1,0:T(8,128)(2,1)S(1)} %fusion.18), channel_id=1, source_target_pairs={{0,8},{8,0},{1,9},{9,1},{2,10},{10,2},{3,11},{11,3},{4,12},{12,4},... | collective-permute-start | bytes 786440 | tf_op jit(solution)/shard_map/ppermute | solution.py:205
  159.1 15.9 %collective-permute-start.28 = (bf16[128,1024]{1,0:T(8,128)(2,1)S(1)}, bf16[128,1024]{1,0:T(8,128)(2,1)S(1)}, u32[]{:S(2)}, u32[]{:S(2)}) collective-permute-start(bf16[128,1024]{1,0:T(8,128)(2,1)S(1)} %fusion.20), channel_id=1, source_target_pairs={{0,8},{8,0},{1,9},{9,1},{2,10},{10,2},{3,11},{11,3},{4,12},{12,4},... | collective-permute-start | bytes 786440 | tf_op jit(solution)/shard_map/ppermute | solution.py:205
  160.0 19.7 %collective-permute-start.21 = (bf16[128,1024]{1,0:T(8,128)(2,1)S(1)}, bf16[128,1024]{1,0:T(8,128)(2,1)S(1)}, u32[]{:S(2)}, u32[]{:S(2)}) collective-permute-start(bf16[128,1024]{1,0:T(8,128)(2,1)S(1)} %fusion.19), channel_id=1, source_target_pairs={{0,8},{8,0},{1,9},{9,1},{2,10},{10,2},{3,11},{11,3},{4,12},{12,4},... | collective-permute-start | bytes 786440 | tf_op jit(solution)/shard_map/ppermute | solution.py:205
  169.5 18.9 %collective-permute-start.36 = (bf16[128,1024]{1,0:T(8,128)(2,1)S(1)}, bf16[128,1024]{1,0:T(8,128)(2,1)S(1)}, u32[]{:S(2)}, u32[]{:S(2)}) collective-permute-start(bf16[128,1024]{1,0:T(8,128)(2,1)S(1)} %fusion.5), channel_id=1, source_target_pairs={{0,4},{1,5},{2,6},{3,7},{4,0},{5,1},{6,2},{7,3},{8,12},{9,13},{10,... | collective-permute-start | bytes 786440 | tf_op jit(solution)/shard_map/ppermute | solution.py:149
  179.8 14.0 %collective-permute-start.22 = (bf16[128,1024]{1,0:T(8,128)(2,1)S(1)}, bf16[128,1024]{1,0:T(8,128)(2,1)S(1)}, u32[]{:S(2)}, u32[]{:S(2)}) collective-permute-start(bf16[128,1024]{1,0:T(8,128)(2,1)S(1)} %fusion.13), channel_id=1, source_target_pairs={{0,6},{1,7},{2,0},{3,1},{4,2},{5,3},{6,4},{7,5},{8,14},{9,15},{10,... | collective-permute-start | bytes 786440 | tf_op jit(solution)/shard_map/ppermute | solution.py:149
  (38 other events, 690.6 us)
